TPU v7x, 32 devices: a whole 2x2x4 slice. The times are simulated.
32 devices in a mesh: pipe: 4 (over z), dp: 2 (over x), tensor: 4 (over y, core).
Axes of the slice: x: 2, y: 2, z: 4, core: 2. Of those that a mesh axis runs over, the one named last changes fastest.
Arguments:
- acts: bfloat16 [4, 4, 128, 8192], P('pipe', None, 'dp', 'tensor'), may hold values from -6 to 6
- w_in: bfloat16 [4, 8192, 512], P('pipe', 'tensor', 'dp'), may hold values from -0.0625 to 0.0625
- w_out: bfloat16 [4, 512, 8192], P('pipe', 'dp', 'tensor'), may hold values from -0.25 to 0.25
- top_grad: bfloat16 [4, 128, 8192], P(None, 'dp', 'tensor'), may hold values from -6 to 6
Outputs:
- grad_input: bfloat16 [4, 4, 128, 8192], P('pipe', None, 'dp', 'tensor')
- grad_w_in: bfloat16 [4, 8192, 512], P('pipe', 'tensor', 'dp')
- grad_w_out: bfloat16 [4, 512, 8192], P('pipe', 'dp', 'tensor')
All inputs are finite; a program needn't handle non-finite values.
Results may differ from a plain program's by a relative error of at most 0.013.
Values may be sent and summed in bfloat16 or wider, within the bound.
A program may use at most 64 MiB of HBM per device.

v0:
```python
import jax
import jax.numpy as jnp
from jax import lax
from jax.sharding import PartitionSpec as P


def shifted(shard, axis, by):
    devices = lax.axis_size(axis)
    pairs = [(i, i + by) for i in range(devices) if 0 <= i + by < devices]
    return lax.ppermute(shard, axis, pairs)


def silu_slope(value):
    sig = jax.nn.sigmoid(value)
    return sig * (1.0 + value * (1.0 - sig))


def put_slot(store, piece, slot, active):
    updated = lax.dynamic_update_index_in_dim(store, piece, slot, 0)
    return jnp.where(active, updated, store)


def shards(acts, w_in, w_out, top_grad):
    pipes = lax.axis_size("pipe")
    section = lax.axis_index("pipe")
    micro = acts.shape[1]
    rows = acts.shape[2]
    width = acts.shape[3]
    saved = acts[0]
    w_in_full, w_out_full = (
        lax.all_gather(w_in[0], "dp", axis=1, tiled=True),
        lax.all_gather(w_out[0], "dp", axis=0, tiled=True),
    )
    inner = w_in_full.shape[1]
    contract = (((1,), (1,)), ((), ()))
    incoming = jnp.zeros((rows, width), jnp.bfloat16)
    dpre_store = jnp.zeros((micro, rows, inner), jnp.bfloat16)
    act_store = jnp.zeros((micro, rows, inner), jnp.bfloat16)
    grad_store = jnp.zeros((micro, rows, width), jnp.bfloat16)
    back_store = jnp.zeros((micro, rows, width), jnp.bfloat16)
    total_steps = micro + pipes - 1
    for step in range(total_steps):
        index = step - (pipes - 1 - section)
        active = jnp.logical_and(index >= 0, index < micro)
        slot = jnp.clip(index, 0, micro - 1)
        top_piece = lax.dynamic_index_in_dim(top_grad, slot, 0, keepdims=False)
        grad_now = jnp.where(section == pipes - 1, top_piece, incoming)
        x_now = lax.dynamic_index_in_dim(saved, slot, 0, keepdims=False)
        pre_part = jnp.dot(x_now, w_in_full, preferred_element_type=jnp.float32)
        pre_now = lax.psum(pre_part, "tensor")
        hidden_part = lax.dot_general(
            grad_now, w_out_full, contract, preferred_element_type=jnp.float32
        )
        hidden = lax.psum(hidden_part, "tensor")
        dpre = (hidden * silu_slope(pre_now)).astype(jnp.bfloat16)
        branch = lax.dot_general(dpre, w_in_full, contract, preferred_element_type=jnp.float32)
        back = (grad_now.astype(jnp.float32) + branch).astype(jnp.bfloat16)
        dpre_store = put_slot(dpre_store, dpre, slot, active)
        act_store = put_slot(act_store, jax.nn.silu(pre_now).astype(jnp.bfloat16), slot, active)
        grad_store = put_slot(grad_store, grad_now, slot, active)
        back_store = put_slot(back_store, back, slot, active)
        if step + 1 < total_steps:
            incoming = shifted(back, "pipe", -1)
    token_dims = (((0,), (0,)), ((), ()))
    flat_x = saved.reshape(micro * rows, width)
    part_in = lax.dot_general(
        flat_x,
        dpre_store.reshape(micro * rows, inner),
        token_dims,
        preferred_element_type=jnp.float32,
    )
    part_out = lax.dot_general(
        act_store.reshape(micro * rows, inner),
        grad_store.reshape(micro * rows, width),
        token_dims,
        preferred_element_type=jnp.float32,
    )
    summed_in, summed_out = (
        lax.psum_scatter(
            part_in.astype(jnp.bfloat16), "dp", scatter_dimension=1, tiled=True
        ).astype(jnp.float32),
        lax.psum_scatter(
            part_out.astype(jnp.bfloat16), "dp", scatter_dimension=0, tiled=True
        ).astype(jnp.float32),
    )
    return (
        back_store[None],
        summed_in.astype(jnp.bfloat16)[None],
        summed_out.astype(jnp.bfloat16)[None],
    )


def solution(mesh):
    placed = (
        P("pipe", None, "dp", "tensor"),
        P("pipe", "tensor", "dp"),
        P("pipe", "dp", "tensor"),
        P(None, "dp", "tensor"),
    )
    return jax.shard_map(
        shards,
        mesh=mesh,
        in_specs=placed,
        out_specs=(
            P("pipe", None, "dp", "tensor"),
            P("pipe", "tensor", "dp"),
            P("pipe", "dp", "tensor"),
        ),
        check_vma=False,
    )
```

profile of v0, /device:TPU:0, one launch (start us, length us, event | category | flops | bytes accessed | tf_op | source)
XLA Modules:
  0.0 486.9 jit_solution(4687135771134606875)
XLA Ops:
  8.7 36.6 %all-gather.7.cloned.1.call-done = bf16[1,2048,512]{2,1,0:T(8,128)(2,1)} async-done(((bf16[1,2048,256]{2,1,0:T(8,128)(2,1)}), bf16[1,2048,512]{2,1,0:T(8,128)(2,1)}) %all-gather.7.cloned.1.call-update) | async-done | bytes 2097168 | tf_op jit(solution)/shard_map/all_gather | solution.py:31
  45.4 2.7 fusion.27
  48.1 32.0 %all-gather.5.cloned.1.call-done = bf16[1,512,2048]{2,1,0:T(8,128)(2,1)} async-done(((bf16[1,256,2048]{2,1,0:T(8,128)(2,1)}), bf16[1,512,2048]{2,1,0:T(8,128)(2,1)}) %all-gather.5.cloned.1.call-update) | async-done | bytes 2097168 | tf_op jit(solution)/shard_map/all_gather | solution.py:32
  80.1 3.1 fusion.41
  84.3 1.7 select_dynamic-update-slice_fusion
  86.0 29.4 %all-reduce.27.cloned.1.call-done = (f32[64,512]{1,0:T(8,128)}, f32[64,512]{1,0:T(8,128)}) async-done(((f32[64,512]{1,0:T(8,128)}, f32[64,512]{1,0:T(8,128)}), (f32[64,512]{1,0:T(8,128)}, f32[64,512]{1,0:T(8,128)})) %all-reduce.27.cloned.1.call-update) | async-done | bytes 262160 | tf_op jit(solution)/shard_map/psum | solution.py:54
  117.6 2.4 bitcast_dynamic-update-slice_fusion
  120.0 1.4 collective-permute-start
  122.6 6.3 %collective-permute-done = bf16[64,2048]{1,0:T(8,128)(2,1)S(1)} collective-permute-done((bf16[64,2048]{1,0:T(8,128)(2,1)S(1)}, bf16[64,2048]{1,0:T(8,128)(2,1)S(1)}, u32[]{:S(2)}, u32[]{:S(2)}) %collective-permute-start) | collective-permute-done | bytes 262176 | tf_op jit(solution)/shard_map/ppermute | solution.py:10
  128.8 1.8 fusion.52
  134.3 30.6 %all-reduce.25.cloned.1.call-done = (f32[64,512]{1,0:T(8,128)}, f32[64,512]{1,0:T(8,128)}) async-done(((f32[64,512]{1,0:T(8,128)}, f32[64,512]{1,0:T(8,128)}), (f32[64,512]{1,0:T(8,128)}, f32[64,512]{1,0:T(8,128)})) %all-reduce.25.cloned.1.call-update) | async-done | bytes 262160 | tf_op jit(solution)/shard_map/psum | solution.py:54
  164.9 1.7 fusion.85
  166.5 2.5 fusion.62
  171.6 6.3 %collective-permute-done.1 = bf16[64,2048]{1,0:T(8,128)(2,1)S(1)} collective-permute-done((bf16[64,2048]{1,0:T(8,128)(2,1)S(1)}, bf16[64,2048]{1,0:T(8,128)(2,1)S(1)}, u32[]{:S(2)}, u32[]{:S(2)}) %collective-permute-start.1) | collective-permute-done | bytes 262176 | tf_op jit(solution)/shard_map/ppermute | solution.py:10
  177.8 1.8 fusion.51
  181.9 32.0 %all-reduce.23.cloned.1.call-done = (f32[64,512]{1,0:T(8,128)}, f32[64,512]{1,0:T(8,128)}) async-done(((f32[64,512]{1,0:T(8,128)}, f32[64,512]{1,0:T(8,128)}), (f32[64,512]{1,0:T(8,128)}, f32[64,512]{1,0:T(8,128)})) %all-reduce.23.cloned.1.call-update) | async-done | bytes 262160 | tf_op jit(solution)/shard_map/psum | solution.py:54
  213.8 1.7 fusion.84
  215.5 2.5 fusion.60
  218.0 1.4 collective-permute-start.2
  220.5 6.3 %collective-permute-done.2 = bf16[64,2048]{1,0:T(8,128)(2,1)S(1)} collective-permute-done((bf16[64,2048]{1,0:T(8,128)(2,1)S(1)}, bf16[64,2048]{1,0:T(8,128)(2,1)S(1)}, u32[]{:S(2)}, u32[]{:S(2)}) %collective-permute-start.2) | collective-permute-done | bytes 262176 | tf_op jit(solution)/shard_map/ppermute | solution.py:10
  226.8 1.8 fusion.50
  230.9 32.0 %all-reduce.21.cloned.1.call-done = (f32[64,512]{1,0:T(8,128)}, f32[64,512]{1,0:T(8,128)}) async-done(((f32[64,512]{1,0:T(8,128)}, f32[64,512]{1,0:T(8,128)}), (f32[64,512]{1,0:T(8,128)}, f32[64,512]{1,0:T(8,128)})) %all-reduce.21.cloned.1.call-update) | async-done | bytes 262160 | tf_op jit(solution)/shard_map/psum | solution.py:54
  262.8 1.7 fusion.83
  264.5 2.5 fusion.58
  267.0 1.4 collective-permute-start.3
  269.6 6.3 %collective-permute-done.3 = bf16[64,2048]{1,0:T(8,128)(2,1)S(1)} collective-permute-done((bf16[64,2048]{1,0:T(8,128)(2,1)S(1)}, bf16[64,2048]{1,0:T(8,128)(2,1)S(1)}, u32[]{:S(2)}, u32[]{:S(2)}) %collective-permute-start.3) | collective-permute-done | bytes 262176 | tf_op jit(solution)/shard_map/ppermute | solution.py:10
  275.8 1.8 fusion.49
  279.9 32.0 %all-reduce.19.cloned.1.call-done = (f32[64,512]{1,0:T(8,128)}, f32[64,512]{1,0:T(8,128)}) async-done(((f32[64,512]{1,0:T(8,128)}, f32[64,512]{1,0:T(8,128)}), (f32[64,512]{1,0:T(8,128)}, f32[64,512]{1,0:T(8,128)})) %all-reduce.19.cloned.1.call-update) | async-done | bytes 262160 | tf_op jit(solution)/shard_map/psum | solution.py:54
  311.8 1.7 fusion.82
  313.5 2.5 fusion.56
  316.0 1.4 collective-permute-start.4
  318.5 6.3 %collective-permute-done.4 = bf16[64,2048]{1,0:T(8,128)(2,1)S(1)} collective-permute-done((bf16[64,2048]{1,0:T(8,128)(2,1)S(1)}, bf16[64,2048]{1,0:T(8,128)(2,1)S(1)}, u32[]{:S(2)}, u32[]{:S(2)}) %collective-permute-start.4) | collective-permute-done | bytes 262176 | tf_op jit(solution)/shard_map/ppermute | solution.py:10
  324.8 1.8 fusion.48
  328.9 32.0 %all-reduce.17.cloned.1.call-done = (f32[64,512]{1,0:T(8,128)}, f32[64,512]{1,0:T(8,128)}) async-done(((f32[64,512]{1,0:T(8,128)}, f32[64,512]{1,0:T(8,128)}), (f32[64,512]{1,0:T(8,128)}, f32[64,512]{1,0:T(8,128)})) %all-reduce.17.cloned.1.call-update) | async-done | bytes 262160 | tf_op jit(solution)/shard_map/psum | solution.py:54
  360.8 1.7 fusion.81
  362.5 2.5 fusion.54
  367.5 6.3 %collective-permute-done.5 = bf16[64,2048]{1,0:T(8,128)(2,1)S(1)} collective-permute-done((bf16[64,2048]{1,0:T(8,128)(2,1)S(1)}, bf16[64,2048]{1,0:T(8,128)(2,1)S(1)}, u32[]{:S(2)}, u32[]{:S(2)}) %collective-permute-start.5) | collective-permute-done | bytes 262176 | tf_op jit(solution)/shard_map/ppermute | solution.py:10
  373.8 1.8 fusion.47
  376.4 1.4 fusion.29
  377.8 32.0 %all-reduce.15.cloned.1.call-done = (f32[64,512]{1,0:T(8,128)}, f32[64,512]{1,0:T(8,128)}) async-done(((f32[64,512]{1,0:T(8,128)}, f32[64,512]{1,0:T(8,128)}), (f32[64,512]{1,0:T(8,128)}, f32[64,512]{1,0:T(8,128)})) %all-reduce.15.cloned.1.call-update) | async-done | bytes 262160 | tf_op jit(solution)/shard_map/psum | solution.py:54
  409.8 1.7 fusion.80
  411.5 2.1 fusion
  413.7 3.4 bitcast_convert_fusion
  417.1 2.3 copy.49
  419.4 2.5 fusion.46
  421.9 23.7 %reduce-scatter.3.cloned.1.call-done = bf16[2048,256]{0,1:T(8,128)(2,1)} async-done(((bf16[2048,512]{0,1:T(8,128)(2,1)}), bf16[2048,256]{0,1:T(8,128)(2,1)}) %reduce-scatter.3.cloned.1.call-update) | async-done | bytes 1048592 | tf_op jit(solution)/shard_map/reduce_scatter | solution.py:79
  445.6 2.3 copy.7
  447.9 32.5 %reduce-scatter.5.cloned.1.call-done = bf16[256,2048]{1,0:T(8,128)(2,1)} async-done(((bf16[512,2048]{1,0:T(8,128)(2,1)}), bf16[256,2048]{1,0:T(8,128)(2,1)}) %reduce-scatter.5.cloned.1.call-update) | async-done | bytes 1048592 | tf_op jit(solution)/shard_map/reduce_scatter | solution.py:82
  (73 shorter events, 27.5 us)
Async XLA Ops:
  7.2 38.2 %copy-start = (bf16[1,4,64,2048]{3,2,1,0:T(8,128)(2,1)S(1)}, bf16[1,4,64,2048]{3,2,1,0:T(8,128)(2,1)}, u32[]{:S(2)}) copy-start(bf16[1,4,64,2048]{3,2,1,0:T(8,128)(2,1)} %param.4) | copy-start | bytes 3145732
  7.2 38.2 %all-gather.7.cloned.1.call-start = ((), (), s32[]{:S(2)}) async-start(), calls=%async_computation.5 | async-start | bytes 3145728 | tf_op jit(solution)/shard_map/all_gather | solution.py:31
  7.9 72.1 %all-gather.5.cloned.1.call-start = ((), (), s32[]{:S(2)}) async-start(), calls=%async_computation.4 | async-start | bytes 3145728 | tf_op jit(solution)/shard_map/all_gather | solution.py:32
  8.7 106.8 %all-reduce.27.cloned.1.call-start = ((), (), s32[]{:S(2)}) async-start(), calls=%async_computation.12 | async-start | bytes 524288 | tf_op jit(solution)/shard_map/psum | solution.py:54
  83.2 34.4 %copy-start.1 = (bf16[1,2048,512]{2,1,0:T(8,128)(2,1)S(1)}, bf16[1,2048,512]{2,1,0:T(8,128)(2,1)}, u32[]{:S(2)}) copy-start(bf16[1,2048,512]{2,1,0:T(8,128)(2,1)} %all-gather.7.cloned.1.call-done) | copy-start | bytes 6291460
  83.2 81.7 %all-reduce.25.cloned.1.call-start = ((), (), s32[]{:S(2)}) async-start(), calls=%async_computation.11 | async-start | bytes 524288 | tf_op jit(solution)/shard_map/psum | solution.py:54
  120.0 11.4 %copy-start.2 = (bf16[1,512,2048]{2,1,0:T(8,128)(2,1)S(1)}, bf16[1,512,2048]{2,1,0:T(8,128)(2,1)}, u32[]{:S(2)}) copy-start(bf16[1,512,2048]{2,1,0:T(8,128)(2,1)} %all-gather.5.cloned.1.call-done) | copy-start | bytes 6291460
  120.0 8.8 %collective-permute-start = (bf16[64,2048]{1,0:T(8,128)(2,1)S(1)}, bf16[64,2048]{1,0:T(8,128)(2,1)S(1)}, u32[]{:S(2)}, u32[]{:S(2)}) collective-permute-start(bf16[64,2048]{1,0:T(8,128)(2,1)S(1)} %get-tuple-element.63), channel_id=1, source_target_pairs={{8,0},{16,8},{24,16},{9,1},{17,9},{25,17},{10,2},{18,10},{26,18},{... | collective-permute-start | bytes 786440 | tf_op jit(solution)/shard_map/ppermute | solution.py:10
  122.6 11.0 %copy-start.15 = (f32[64,512]{1,0:T(8,128)S(1)}, f32[64,512]{1,0:T(8,128)}, u32[]{:S(2)}) copy-start(f32[64,512]{1,0:T(8,128)} %get-tuple-element.19) | copy-start | bytes 393220
  130.7 0.7 copy-start.12
  132.8 81.0 %all-reduce.23.cloned.1.call-start = ((), (), s32[]{:S(2)}) async-start(), calls=%async_computation.10 | async-start | bytes 524288 | tf_op jit(solution)/shard_map/psum | solution.py:54
  169.0 11.4 %copy-start.3 = (bf16[1,512,2048]{2,1,0:T(8,128)(2,1)S(1)}, bf16[1,512,2048]{2,1,0:T(8,128)(2,1)}, u32[]{:S(2)}) copy-start(bf16[1,512,2048]{2,1,0:T(8,128)(2,1)} %all-gather.5.cloned.1.call-done) | copy-start | bytes 6291460
  169.0 8.8 %collective-permute-start.1 = (bf16[64,2048]{1,0:T(8,128)(2,1)S(1)}, bf16[64,2048]{1,0:T(8,128)(2,1)S(1)}, u32[]{:S(2)}, u32[]{:S(2)}) collective-permute-start(bf16[64,2048]{1,0:T(8,128)(2,1)S(1)} %get-tuple-element.55), channel_id=1, source_target_pairs={{8,0},{16,8},{24,16},{9,1},{17,9},{25,17},{10,2},{18,10},{26,18},{... | collective-permute-start | bytes 786440 | tf_op jit(solution)/shard_map/ppermute | solution.py:10
  179.7 0.7 copy-start.11
  181.8 81.0 %all-reduce.21.cloned.1.call-start = ((), (), s32[]{:S(2)}) async-start(), calls=%async_computation.9 | async-start | bytes 524288 | tf_op jit(solution)/shard_map/psum | solution.py:54
  218.0 11.4 %copy-start.4 = (bf16[1,512,2048]{2,1,0:T(8,128)(2,1)S(1)}, bf16[1,512,2048]{2,1,0:T(8,128)(2,1)}, u32[]{:S(2)}) copy-start(bf16[1,512,2048]{2,1,0:T(8,128)(2,1)} %all-gather.5.cloned.1.call-done) | copy-start | bytes 6291460
  218.0 8.8 %collective-permute-start.2 = (bf16[64,2048]{1,0:T(8,128)(2,1)S(1)}, bf16[64,2048]{1,0:T(8,128)(2,1)S(1)}, u32[]{:S(2)}, u32[]{:S(2)}) collective-permute-start(bf16[64,2048]{1,0:T(8,128)(2,1)S(1)} %get-tuple-element.53), channel_id=1, source_target_pairs={{8,0},{16,8},{24,16},{9,1},{17,9},{25,17},{10,2},{18,10},{26,18},{... | collective-permute-start | bytes 786440 | tf_op jit(solution)/shard_map/ppermute | solution.py:10
  228.7 0.7 copy-start.10
  230.8 81.0 %all-reduce.19.cloned.1.call-start = ((), (), s32[]{:S(2)}) async-start(), calls=%async_computation.8 | async-start | bytes 524288 | tf_op jit(solution)/shard_map/psum | solution.py:54
  267.0 11.4 %copy-start.5 = (bf16[1,512,2048]{2,1,0:T(8,128)(2,1)S(1)}, bf16[1,512,2048]{2,1,0:T(8,128)(2,1)}, u32[]{:S(2)}) copy-start(bf16[1,512,2048]{2,1,0:T(8,128)(2,1)} %all-gather.5.cloned.1.call-done) | copy-start | bytes 6291460
  267.0 8.8 %collective-permute-start.3 = (bf16[64,2048]{1,0:T(8,128)(2,1)S(1)}, bf16[64,2048]{1,0:T(8,128)(2,1)S(1)}, u32[]{:S(2)}, u32[]{:S(2)}) collective-permute-start(bf16[64,2048]{1,0:T(8,128)(2,1)S(1)} %get-tuple-element.51), channel_id=1, source_target_pairs={{8,0},{16,8},{24,16},{9,1},{17,9},{25,17},{10,2},{18,10},{26,18},{... | collective-permute-start | bytes 786440 | tf_op jit(solution)/shard_map/ppermute | solution.py:10
  277.7 0.7 copy-start.9
  279.8 81.0 %all-reduce.17.cloned.1.call-start = ((), (), s32[]{:S(2)}) async-start(), calls=%async_computation.7 | async-start | bytes 524288 | tf_op jit(solution)/shard_map/psum | solution.py:54
  316.0 11.4 %copy-start.6 = (bf16[1,512,2048]{2,1,0:T(8,128)(2,1)S(1)}, bf16[1,512,2048]{2,1,0:T(8,128)(2,1)}, u32[]{:S(2)}) copy-start(bf16[1,512,2048]{2,1,0:T(8,128)(2,1)} %all-gather.5.cloned.1.call-done) | copy-start | bytes 6291460
  316.0 8.8 %collective-permute-start.4 = (bf16[64,2048]{1,0:T(8,128)(2,1)S(1)}, bf16[64,2048]{1,0:T(8,128)(2,1)S(1)}, u32[]{:S(2)}, u32[]{:S(2)}) collective-permute-start(bf16[64,2048]{1,0:T(8,128)(2,1)S(1)} %get-tuple-element.49), channel_id=1, source_target_pairs={{8,0},{16,8},{24,16},{9,1},{17,9},{25,17},{10,2},{18,10},{26,18},{... | collective-permute-start | bytes 786440 | tf_op jit(solution)/shard_map/ppermute | solution.py:10
  326.7 0.7 copy-start.8
  328.8 81.0 %all-reduce.15.cloned.1.call-start = ((), (), s32[]{:S(2)}) async-start(), calls=%async_computation.6 | async-start | bytes 524288 | tf_op jit(solution)/shard_map/psum | solution.py:54
  365.0 11.4 %copy-start.7 = (bf16[1,512,2048]{2,1,0:T(8,128)(2,1)S(1)}, bf16[1,512,2048]{2,1,0:T(8,128)(2,1)}, u32[]{:S(2)}) copy-start(bf16[1,512,2048]{2,1,0:T(8,128)(2,1)} %all-gather.5.cloned.1.call-done) | copy-start | bytes 6291460
  365.0 8.8 %collective-permute-start.5 = (bf16[64,2048]{1,0:T(8,128)(2,1)S(1)}, bf16[64,2048]{1,0:T(8,128)(2,1)S(1)}, u32[]{:S(2)}, u32[]{:S(2)}) collective-permute-start(bf16[64,2048]{1,0:T(8,128)(2,1)S(1)} %get-tuple-element.47), channel_id=1, source_target_pairs={{8,0},{16,8},{24,16},{9,1},{17,9},{25,17},{10,2},{18,10},{26,18},{... | collective-permute-start | bytes 786440 | tf_op jit(solution)/shard_map/ppermute | solution.py:10
  375.7 0.7 copy-start.13
  377.8 67.8 %reduce-scatter.3.cloned.1.call-start = ((), (), s32[]{:S(2)}) async-start(), calls=%async_computation.2 | async-start | bytes 3145728 | tf_op jit(solution)/shard_map/reduce_scatter | solution.py:79
  413.6 66.8 %reduce-scatter.5.cloned.1.call-start = ((), (), s32[]{:S(2)}) async-start(), calls=%async_computation.3 | async-start | bytes 3145728 | tf_op jit(solution)/shard_map/reduce_scatter | solution.py:82
  417.1 2.4 copy-start.14
Sparse Core Ops, SparseCore 0:
  9.5 35.7 all-gather.6
  46.9 33.1 all-gather.4
  83.3 32.0 all-reduce.26
  132.9 31.8 all-reduce.24
  181.9 31.8 all-reduce.22
  230.9 31.8 all-reduce.20
  279.9 31.8 all-reduce.18
  328.9 31.8 all-reduce.16
  377.9 31.8 all-reduce.14
  413.7 31.8 reduce-scatter.2
  448.4 31.8 reduce-scatter.4
where the time goes:
time: 488 us; the launch traced here: 487 us
  waiting for transfers between devices  384 us (79%)
  matrix products  44 us (9%)
  other arithmetic  24.4 us (5%)
  between operations  14 us (3%)
  local copies, waits for them, and re-layouts  11.8 us (2%)
  starting transfers between devices  8.92 us (2%)
    psum x7, waiting for transfers between devices, shards(): hidden = lax.psum(hidden_part, 'tensor')  220 us
    ppermute x6, waiting for transfers between devices, shifted(): return lax.ppermute(shard, axis, pairs)  37.7 us
    all_gather x1, waiting for transfers between devices, shards(): lax.all_gather(w_in[0], 'dp', axis=1, tiled=True)  36.6 us
    reduce_scatter x1, waiting for transfers between devices, shards(): lax.psum_scatter(part_out.astype(jnp.bfloat16), 'dp', scatter_dimension=0...  32.5 us
    all_gather x1, waiting for transfers between devices, shards(): lax.all_gather(w_out[0], 'dp', axis=0, tiled=True)  32 us
    select_n x15, other arithmetic, put_slot(): return jnp.where(active, updated, store)  24.4 us
    reduce_scatter x1, waiting for transfers between devices, shards(): lax.psum_scatter(part_in.astype(jnp.bfloat16), 'dp', scatter_dimension=1,...  23.7 us
    dot_general x7, matrix products, shards(): lax.dot_general(dpre, w_in_full, contract, preferred_element_type=jnp.flo...  17.4 us
  transfers between devices with their start and end apart: 17, of which 17 were waited for; matrix products, arithmetic and copies ran while one was open for 5% of the time, Pallas kernels for 0%

commit v1 on v0

v1 whole, which is shorter than its diff:
```python
import functools

import jax
import jax.numpy as jnp
from jax import lax
from jax.experimental import pallas as pl
from jax.experimental.pallas import tpu as pltpu
from jax.sharding import PartitionSpec as P

MESH = pl.DeviceIdType.MESH
LAST = (((1,), (1,)), ((), ()))
FIRST = (((0,), (0,)), ((), ()))


def silu_slope(value):
    sig = jax.nn.sigmoid(value)
    return sig * (1.0 + value * (1.0 - sig))


def dot(left, right, dims):
    return lax.dot_general(left, right, dims, preferred_element_type=jnp.float32)


def chain(
    pipes, parts, chunks,
    x_ref, wi_ref, wo_ref, top_ref,
    back_ref, pin_ref, pout_ref,
    g_buf, pre_send, pre_recv, act_buf, hid_send, hid_recv, dpre_buf, slope_buf,
    pre_ss, pre_rs, act_ss, act_rs, hid_ss, hid_rs, dp_ss, dp_rs, g_ss, g_rs,
):
    micro, rows, width = x_ref.shape
    inner = wi_ref.shape[1]
    quarter = inner // parts
    step_w = width // chunks
    section = lax.axis_index("pipe")
    me = lax.axis_index("tensor")
    first = section == pipes - 1
    below = jnp.maximum(section - 1, 0)
    above = jnp.minimum(section + 1, pipes - 1)
    peers = [lax.rem(me + d, parts) for d in range(1, parts)]

    barrier = pltpu.get_barrier_semaphore()
    for peer in peers:
        pl.semaphore_signal(barrier, inc=1, device_id={"tensor": peer}, device_id_type=MESH)

    @pl.when(section > 0)
    def _():
        pl.semaphore_signal(barrier, inc=1, device_id={"pipe": below}, device_id_type=MESH)

    @pl.when(section < pipes - 1)
    def _():
        pl.semaphore_signal(barrier, inc=1, device_id={"pipe": above}, device_id_type=MESH)

    beside = jnp.minimum(section, 1) + jnp.minimum(pipes - 1 - section, 1)
    pl.semaphore_wait(barrier, parts - 1 + beside)

    def remote(src, dst, send, recv, where):
        return pltpu.make_async_remote_copy(
            src_ref=src, dst_ref=dst, send_sem=send, recv_sem=recv,
            device_id=where, device_id_type=MESH,
        )

    @pl.when(first)
    def _():
        g_buf[...] = top_ref[...]

    flat_x = x_ref[...].reshape(micro * rows, width)
    pre = jnp.dot(flat_x, wi_ref[...], preferred_element_type=jnp.float32)
    for t in range(parts):
        pre_send[t] = pre[:, t * quarter : (t + 1) * quarter]
    pre_copies = [
        remote(pre_send.at[peer], pre_recv.at[d], pre_ss.at[d], pre_rs.at[d], {"tensor": peer})
        for d, peer in enumerate(peers)
    ]
    for copy in pre_copies:
        copy.start()

    hid_copies = [
        [
            remote(hid_send.at[m, peer], hid_recv.at[m, d], hid_ss.at[m, d], hid_rs.at[m, d], {"tensor": peer})
            for d, peer in enumerate(peers)
        ]
        for m in range(micro)
    ]
    dp_copies = [
        [
            remote(dpre_buf.at[m, me], dpre_buf.at[m, me], dp_ss.at[m, d], dp_rs.at[m, d], {"tensor": peer})
            for d, peer in enumerate(peers)
        ]
        for m in range(micro)
    ]
    act_copies = [
        remote(act_buf.at[me], act_buf.at[me], act_ss.at[d], act_rs.at[d], {"tensor": peer})
        for d, peer in enumerate(peers)
    ]
    g_copies = [
        [
            remote(
                back_ref.at[m, :, pl.ds(c * step_w, step_w)], g_buf.at[m, :, pl.ds(c * step_w, step_w)],
                g_ss.at[m, c], g_rs.at[m, c], {"pipe": below},
            )
            for c in range(chunks)
        ]
        for m in range(micro)
    ]

    def hidden_start(m):
        @pl.when(section < pipes - 1)
        def _():
            for copy in g_copies[m]:
                copy.wait_recv()

        part = dot(g_buf[m], wo_ref[...], LAST)
        for t in range(parts):
            hid_send[m, t] = part[:, t * quarter : (t + 1) * quarter]
        for copy in hid_copies[m]:
            copy.start()

    hidden_start(0)
    for copy in pre_copies:
        copy.wait_recv()
    mine = pre_send[me]
    for d in range(parts - 1):
        mine = mine + pre_recv[d]
    slope_buf[...] = silu_slope(mine)
    act_buf[me] = jax.nn.silu(mine).astype(jnp.bfloat16)
    for copy in act_copies:
        copy.start()

    for m in range(micro):
        if m > 0:
            hidden_start(m)
        for copy in hid_copies[m]:
            copy.wait_recv()
        hidden = hid_send[m, me]
        for d in range(parts - 1):
            hidden = hidden + hid_recv[m, d]
        dpre_buf[m, me] = (hidden * slope_buf[m * rows : (m + 1) * rows, :]).astype(jnp.bfloat16)
        for copy in dp_copies[m]:
            copy.start()
        for copy in dp_copies[m]:
            copy.wait_recv()
        dpre = jnp.concatenate([dpre_buf[m, t] for t in range(parts)], axis=1)
        for c in range(chunks):
            cols = pl.ds(c * step_w, step_w)
            branch = dot(dpre, wi_ref[cols, :], LAST)
            back_ref[m, :, cols] = (g_buf[m, :, cols].astype(jnp.float32) + branch).astype(jnp.bfloat16)

            @pl.when(section > 0)
            def _():
                g_copies[m][c].start()

    for copy in act_copies:
        copy.wait_recv()
    act = jnp.concatenate([act_buf[t] for t in range(parts)], axis=1)
    dpre = jnp.concatenate(
        [dpre_buf[:, t].reshape(micro * rows, quarter) for t in range(parts)], axis=1
    )

    def grads(c, carry):
        cols = pl.ds(pl.multiple_of(c * step_w, step_w), step_w)
        x_cols = x_ref[:, :, cols].reshape(micro * rows, step_w)
        g_cols = g_buf[:, :, cols].reshape(micro * rows, step_w)
        pin_ref[cols, :] = dot(x_cols, dpre, FIRST).astype(jnp.bfloat16)
        pout_ref[:, cols] = dot(act, g_cols, FIRST).astype(jnp.bfloat16)
        return carry

    lax.fori_loop(0, chunks, grads, 0)

    for copy in pre_copies + act_copies:
        copy.wait_send()
    for m in range(micro):
        for copy in hid_copies[m] + dp_copies[m]:
            copy.wait_send()

        @pl.when(section > 0)
        def _():
            for copy in g_copies[m]:
                copy.wait_send()


def shards(acts, w_in, w_out, top_grad):
    pipes = lax.axis_size("pipe")
    parts = lax.axis_size("tensor")
    saved = acts[0]
    micro, rows, width = saved.shape
    w_in_full = lax.all_gather(w_in[0], "dp", axis=1, tiled=True)
    w_out_full = lax.all_gather(w_out[0], "dp", axis=0, tiled=True)
    inner = w_in_full.shape[1]
    quarter = inner // parts
    chunks = 4
    others = parts - 1
    bf, f32 = jnp.bfloat16, jnp.float32
    dma = pltpu.SemaphoreType.DMA
    vmem = pl.BlockSpec(memory_space=pltpu.VMEM)
    back, part_in, part_out = pl.pallas_call(
        functools.partial(chain, pipes, parts, chunks),
        out_shape=(
            jax.ShapeDtypeStruct((micro, rows, width), bf),
            jax.ShapeDtypeStruct((width, inner), bf),
            jax.ShapeDtypeStruct((inner, width), bf),
        ),
        in_specs=[vmem] * 4,
        out_specs=(vmem,) * 3,
        scratch_shapes=[
            pltpu.VMEM((micro, rows, width), bf),
            pltpu.VMEM((parts, micro * rows, quarter), f32),
            pltpu.VMEM((others, micro * rows, quarter), f32),
            pltpu.VMEM((parts, micro * rows, quarter), bf),
            pltpu.VMEM((micro, parts, rows, quarter), f32),
            pltpu.VMEM((micro, others, rows, quarter), f32),
            pltpu.VMEM((micro, parts, rows, quarter), bf),
            pltpu.VMEM((micro * rows, quarter), f32),
            dma((others,)), dma((others,)), dma((others,)), dma((others,)),
            dma((micro, others)), dma((micro, others)),
            dma((micro, others)), dma((micro, others)),
            dma((micro, chunks)), dma((micro, chunks)),
        ],
        compiler_params=pltpu.CompilerParams(
            collective_id=0, has_side_effects=True, vmem_limit_bytes=48 * 1024 * 1024
        ),
    )(saved, w_in_full, w_out_full, top_grad)
    grad_in = lax.psum_scatter(part_in, "dp", scatter_dimension=1, tiled=True)
    grad_out = lax.psum_scatter(part_out, "dp", scatter_dimension=0, tiled=True)
    return back[None], grad_in[None], grad_out[None]


def solution(mesh):
    placed = (
        P("pipe", None, "dp", "tensor"),
        P("pipe", "tensor", "dp"),
        P("pipe", "dp", "tensor"),
        P(None, "dp", "tensor"),
    )
    return jax.shard_map(
        shards,
        mesh=mesh,
        in_specs=placed,
        out_specs=(
            P("pipe", None, "dp", "tensor"),
            P("pipe", "tensor", "dp"),
            P("pipe", "dp", "tensor"),
        ),
        check_vma=False,
    )
```

time: 488 us -> 245 us (0.50)
  waiting for transfers between devices: 384 us -> 136 us
  Pallas kernels: 0 us -> 93.3 us
  matrix products: 44 us -> 0 us
  other arithmetic: 24.4 us -> 0 us
  local copies, waits for them, and re-layouts: 11.8 us -> 0.98 us
  starting transfers between devices: 8.92 us -> 0.16 us
    psum x7 -> x0, waiting for transfers between devices: 220 us -> none  [shards(): hidden = lax.psum(hidden_part, 'tensor')]
    pallas_call x0 -> x1, Pallas kernels: none -> 93.3 us  [shards(): pl.pallas_call(functools.partial(chain, pipes, parts, chunks), out_shape=...]
    dot_general x23 -> x0, matrix products: 44 us -> none  [the longest x7 17.4 us: shards(): lax.dot_general(dpre, w_in_full, contract, preferred_element_type=jnp.flo...]
    ppermute x6 -> x0, waiting for transfers between devices: 37.7 us -> none  [shifted(): return lax.ppermute(shard, axis, pairs)]
    select_n x15 -> x0, other arithmetic: 24.4 us -> none  [put_slot(): return jnp.where(active, updated, store)]
    ppermute x6 -> x0, starting transfers between devices: 8.47 us -> none  [shifted(): return lax.ppermute(shard, axis, pairs)]
    unnamed x34 -> x5, local copies, waits for them, and re-layouts: 8.85 us -> 0.98 us
    reduce_scatter x2, waiting for transfers between devices: 56.2 us -> 62.9 us  [the longest x1 34.6 us: shards(): grad_out = lax.psum_scatter(part_out, 'dp', scatter_dimension=0, tiled=True)]
  transfers between devices with their start and end apart: 17 -> 4, of which waited for: 17 -> 4; matrix products, arithmetic and copies ran while one was open for 5% -> 0% of each run, Pallas kernels for 0% -> 0%
where the time goes in v1:
time: 245 us; the launch traced here: 244 us
  waiting for transfers between devices  136 us (56%)
  Pallas kernels  93.3 us (38%)
  between operations  13.8 us (6%)
    pallas_call x1, Pallas kernels, shards(): pl.pallas_call(functools.partial(chain, pipes, parts, chunks), out_shape=...  93.3 us
    all_gather x1, waiting for transfers between devices, shards(): w_in_full = lax.all_gather(w_in[0], 'dp', axis=1, tiled=True)  36.7 us
    all_gather x1, waiting for transfers between devices, shards(): w_out_full = lax.all_gather(w_out[0], 'dp', axis=0, tiled=True)  34.7 us
    reduce_scatter x1, waiting for transfers between devices, shards(): grad_out = lax.psum_scatter(part_out, 'dp', scatter_dimension=0, tiled=True)  34.6 us
    reduce_scatter x1, waiting for transfers between devices, shards(): grad_in = lax.psum_scatter(part_in, 'dp', scatter_dimension=1, tiled=True)  28.3 us
  transfers between devices with their start and end apart: 4, of which 4 were waited for; matrix products, arithmetic and copies ran while one was open for 0% of the time, Pallas kernels for 0%

profile of v1, /device:TPU:0, one launch (start us, length us, event | category | flops | bytes accessed | tf_op | source)
XLA Modules:
  0.0 244.4 jit_solution(8269441619456008642)
XLA Ops:
  7.2 0.0 copy-start.1
  7.2 0.0 copy-start
  7.2 0.0 all-gather.5.cloned.1.call-start
  7.2 0.7 all-gather.5.cloned.1.call-update
  7.9 0.0 all-gather.7.cloned.1.call-start
  8.0 0.7 all-gather.7.cloned.1.call-update
  8.7 0.0 reduce-scatter.3.cloned.1.call-start
  8.7 36.7 %all-gather.5.cloned.1.call-done = bf16[1,2048,512]{2,1,0:T(8,128)(2,1)} async-done(((bf16[1,2048,256]{2,1,0:T(8,128)(2,1)}), bf16[1,2048,512]{2,1,0:T(8,128)(2,1)}) %all-gather.5.cloned.1.call-update) | async-done | bytes 2097168 | tf_op jit(solution)/shard_map/all_gather | solution.py:187
  45.4 34.7 %all-gather.7.cloned.1.call-done = bf16[1,512,2048]{2,1,0:T(8,128)(2,1)} async-done(((bf16[1,256,2048]{2,1,0:T(8,128)(2,1)}), bf16[1,512,2048]{2,1,0:T(8,128)(2,1)}) %all-gather.7.cloned.1.call-update) | async-done | bytes 2097168 | tf_op jit(solution)/shard_map/all_gather | solution.py:188
  80.1 0.0 copy-done.1
  80.1 0.0 copy-done
  80.1 93.3 %shard_map.67 = (bf16[4,64,2048]{2,1,0:T(8,128)(2,1)S(1)}, bf16[2048,512]{1,0:T(8,128)(2,1)}, bf16[512,2048]{1,0:T(8,128)(2,1)}) custom-call(bf16[4,64,2048]{2,1,0:T(8,128)(2,1)S(1)} %bitcast.7, bf16[2048,512]{1,0:T(8,128)(2,1)} %bitcast.8, bf16[512,2048]{1,0:T(8,128)(2,1)} %bitcast.9, bf16[4,64,2048]{2,1,0:T(8,128)(2,1)S(1)} %copy-done.1), custom_call_target="tpu_custom_call" | custom-call | tf_op jit(solution)/shard_map/pallas_call | solution.py:196
  173.4 0.0 reduce-scatter.3.cloned.1.call-update
  173.4 0.0 reduce-scatter.5.cloned.1.call-start
  173.5 0.5 reduce-scatter.5.cloned.1.call-update
  174.0 28.3 %reduce-scatter.3.cloned.1.call-done = bf16[2048,256]{1,0:T(8,128)(2,1)} async-done(((bf16[2048,512]{1,0:T(8,128)(2,1)}), bf16[2048,256]{1,0:T(8,128)(2,1)}) %reduce-scatter.3.cloned.1.call-update) | async-done | bytes 1048592 | tf_op jit(solution)/shard_map/reduce_scatter | solution.py:223
  202.3 34.6 %reduce-scatter.5.cloned.1.call-done = bf16[256,2048]{1,0:T(8,128)(2,1)} async-done(((bf16[512,2048]{1,0:T(8,128)(2,1)}), bf16[256,2048]{1,0:T(8,128)(2,1)}) %reduce-scatter.5.cloned.1.call-update) | async-done | bytes 1048592 | tf_op jit(solution)/shard_map/reduce_scatter | solution.py:224
  236.9 1.0 copy.8
Async XLA Ops:
  7.2 72.9 %copy-start.1 = (bf16[4,64,2048]{2,1,0:T(8,128)(2,1)S(1)}, bf16[4,64,2048]{2,1,0:T(8,128)(2,1)}, u32[]{:S(2)}) copy-start(bf16[4,64,2048]{2,1,0:T(8,128)(2,1)} %top_ref.1) | copy-start | bytes 3145732
  7.2 72.9 %copy-start = (bf16[1,4,64,2048]{3,2,1,0:T(8,128)(2,1)S(1)}, bf16[1,4,64,2048]{3,2,1,0:T(8,128)(2,1)}, u32[]{:S(2)}) copy-start(bf16[1,4,64,2048]{3,2,1,0:T(8,128)(2,1)} %param.4) | copy-start | bytes 3145732
  7.2 38.2 %all-gather.5.cloned.1.call-start = ((), (), s32[]{:S(2)}) async-start(), calls=%async_computation.4 | async-start | bytes 3145728 | tf_op jit(solution)/shard_map/all_gather | solution.py:187
  7.9 72.1 %all-gather.7.cloned.1.call-start = ((), (), s32[]{:S(2)}) async-start(), calls=%async_computation.5 | async-start | bytes 3145728 | tf_op jit(solution)/shard_map/all_gather | solution.py:188
  8.7 193.6 %reduce-scatter.3.cloned.1.call-start = ((), (), s32[]{:S(2)}) async-start(), calls=%async_computation.2 | async-start | bytes 3145728 | tf_op jit(solution)/shard_map/reduce_scatter | solution.py:223
  173.4 63.4 %reduce-scatter.5.cloned.1.call-start = ((), (), s32[]{:S(2)}) async-start(), calls=%async_computation.3 | async-start | bytes 3145728 | tf_op jit(solution)/shard_map/reduce_scatter | solution.py:224
Sparse Core Ops, SparseCore 0:
  9.6 35.7 all-gather.4
  46.9 33.1 all-gather.6
  173.5 28.6 reduce-scatter.2
  205.0 31.8 reduce-scatter.4

commit v2 on v1

v2 whole, which is shorter than its diff:
```python
import functools

import jax
import jax.numpy as jnp
from jax import lax
from jax.experimental import pallas as pl
from jax.experimental.pallas import tpu as pltpu
from jax.sharding import PartitionSpec as P

MESH = pl.DeviceIdType.MESH
LAST = (((1,), (1,)), ((), ()))
FIRST = (((0,), (0,)), ((), ()))


def silu_slope(value):
    sig = jax.nn.sigmoid(value)
    return sig * (1.0 + value * (1.0 - sig))


def dot(left, right, dims):
    return lax.dot_general(left, right, dims, preferred_element_type=jnp.float32)


def chain(
    pipes, parts, pair, chunks,
    x_ref, wi_ref, wo_ref, top_ref,
    back_ref, pin_ref, pout_ref,
    g_buf, pre_send, pre_recv, act_buf, hid_send, hid_recv, dpre_buf, slope_buf,
    pre_ss, pre_rs, act_ss, act_rs, hid_ss, hid_rs, dp_ss, dp_rs, g_ss, g_rs,
    *across,
):
    micro, rows, width = x_ref.shape
    own = wi_ref.shape[1]
    halves = 2 if pair else 1
    per = parts // halves
    quarter = own // per
    step_w = width // chunks
    section = lax.axis_index("pipe")
    me = lax.axis_index("tensor")
    first = section == pipes - 1
    below = jnp.maximum(section - 1, 0)
    above = jnp.minimum(section + 1, pipes - 1)
    peers = [lax.rem(me + d, parts) for d in range(1, parts)]

    barrier = pltpu.get_barrier_semaphore()
    for peer in peers:
        pl.semaphore_signal(barrier, inc=1, device_id={"tensor": peer}, device_id_type=MESH)
    if pair:
        partner = {"dp": 1 - lax.axis_index("dp")}
        pl.semaphore_signal(barrier, inc=1, device_id=partner, device_id_type=MESH)

    @pl.when(section > 0)
    def _():
        pl.semaphore_signal(barrier, inc=1, device_id={"pipe": below}, device_id_type=MESH)

    @pl.when(section < pipes - 1)
    def _():
        pl.semaphore_signal(barrier, inc=1, device_id={"pipe": above}, device_id_type=MESH)

    beside = jnp.minimum(section, 1) + jnp.minimum(pipes - 1 - section, 1)
    pl.semaphore_wait(barrier, parts - 1 + halves - 1 + beside)

    def remote(src, dst, send, recv, where):
        return pltpu.make_async_remote_copy(
            src_ref=src, dst_ref=dst, send_sem=send, recv_sem=recv,
            device_id=where, device_id_type=MESH,
        )

    wi_halves, wo_halves = [wi_ref], [wo_ref]
    if pair:
        wi_other, wo_other, x_other, g_other, dpre_other, act_other, one_ss, one_rs, gx_ss, gx_rs, dx_ss, dx_rs = across
        wi_halves.append(wi_other)
        wo_halves.append(wo_other)
        wi_copy = remote(wi_ref, wi_other, one_ss.at[0], one_rs.at[0], partner)
        wo_copy = remote(wo_ref, wo_other, one_ss.at[1], one_rs.at[1], partner)
        x_copy = remote(x_ref, x_other, one_ss.at[2], one_rs.at[2], partner)
        actx_copy = remote(act_buf.at[pl.ds(per, per)], act_other, one_ss.at[3], one_rs.at[3], partner)
        gx_copies = [remote(g_buf.at[m], g_other.at[m], gx_ss.at[m], gx_rs.at[m], partner) for m in range(micro)]
        dx_copies = [
            remote(dpre_buf.at[m, pl.ds(per, per)], dpre_other.at[m], dx_ss.at[m], dx_rs.at[m], partner)
            for m in range(micro)
        ]
        wi_copy.start()

    @pl.when(first)
    def _():
        g_buf[...] = top_ref[...]

    pre_copies = [
        remote(pre_send.at[peer], pre_recv.at[d], pre_ss.at[d], pre_rs.at[d], {"tensor": peer})
        for d, peer in enumerate(peers)
    ]
    hid_copies = [
        [
            remote(hid_send.at[m, peer], hid_recv.at[m, d], hid_ss.at[m, d], hid_rs.at[m, d], {"tensor": peer})
            for d, peer in enumerate(peers)
        ]
        for m in range(micro)
    ]
    dp_copies = [
        [
            remote(dpre_buf.at[m, me], dpre_buf.at[m, me], dp_ss.at[m, d], dp_rs.at[m, d], {"tensor": peer})
            for d, peer in enumerate(peers)
        ]
        for m in range(micro)
    ]
    act_copies = [
        remote(act_buf.at[me], act_buf.at[me], act_ss.at[d], act_rs.at[d], {"tensor": peer})
        for d, peer in enumerate(peers)
    ]
    g_copies = [
        [
            remote(
                back_ref.at[m, :, pl.ds(c * step_w, step_w)], g_buf.at[m, :, pl.ds(c * step_w, step_w)],
                g_ss.at[m, c], g_rs.at[m, c], {"pipe": below},
            )
            for c in range(chunks)
        ]
        for m in range(micro)
    ]

    flat_x = x_ref[...].reshape(micro * rows, width)
    for h in range(halves):
        if h == 1:
            wi_copy.wait_recv()
            wo_copy.start()
        pre = jnp.dot(flat_x, wi_halves[h][...], preferred_element_type=jnp.float32)
        for t in range(per):
            pre_send[h * per + t] = pre[:, t * quarter : (t + 1) * quarter]
    for copy in pre_copies:
        copy.start()

    def hidden_now(which):
        count = len(which)
        g_now = g_buf[which[0] : which[-1] + 1].reshape(count * rows, width)
        for h in range(halves):
            part = dot(g_now, wo_halves[h][...], LAST)
            for t in range(per):
                for i, m in enumerate(which):
                    hid_send[m, h * per + t] = part[i * rows : (i + 1) * rows, t * quarter : (t + 1) * quarter]
        for m in which:
            for copy in hid_copies[m]:
                copy.start()
        if pair:
            for m in which:
                gx_copies[m].start()

    def dpre_now(m):
        for copy in hid_copies[m]:
            copy.wait_recv()
        hidden = hid_send[m, me]
        for d in range(parts - 1):
            hidden = hidden + hid_recv[m, d]
        dpre_buf[m, me] = (hidden * slope_buf[m * rows : (m + 1) * rows, :]).astype(jnp.bfloat16)
        for copy in dp_copies[m]:
            copy.start()

    for copy in pre_copies:
        copy.wait_recv()
    mine = pre_send[me]
    for d in range(parts - 1):
        mine = mine + pre_recv[d]
    slope_buf[...] = silu_slope(mine)
    act_buf[me] = jax.nn.silu(mine).astype(jnp.bfloat16)
    for copy in act_copies:
        copy.start()

    if pair:
        wo_copy.wait_recv()
        x_copy.start()

    @pl.when(first)
    def _():
        hidden_now(list(range(micro)))
        for m in range(micro):
            dpre_now(m)

    for m in range(micro):
        @pl.when(section < pipes - 1)
        def _():
            for copy in g_copies[m]:
                copy.wait_recv()
            hidden_now([m])
            dpre_now(m)

        for copy in dp_copies[m]:
            copy.wait_recv()
        dpre_halves = [
            jnp.concatenate([dpre_buf[m, h * per + t] for t in range(per)], axis=1) for h in range(halves)
        ]
        for c in range(chunks):
            cols = pl.ds(c * step_w, step_w)
            total = g_buf[m, :, cols].astype(jnp.float32)
            for h in range(halves):
                total = total + dot(dpre_halves[h], wi_halves[h][cols, :], LAST)
            back_ref[m, :, cols] = total.astype(jnp.bfloat16)

            @pl.when(section > 0)
            def _():
                g_copies[m][c].start()

        if pair:
            dx_copies[m].start()
        if m == 0:
            for copy in act_copies:
                copy.wait_recv()
            if pair:
                actx_copy.start()

    sources = [(x_ref, g_buf, act_buf, dpre_buf)]
    if pair:
        x_copy.wait_recv()
        actx_copy.wait_recv()
        for m in range(micro):
            gx_copies[m].wait_recv()
            dx_copies[m].wait_recv()
        sources.append((x_other, g_other, act_other, dpre_other))
    ready = []
    for x_from, g_from, act_from, dpre_from in sources:
        act = jnp.concatenate([act_from[t] for t in range(per)], axis=1)
        dpre = jnp.concatenate(
            [dpre_from[:, t].reshape(micro * rows, quarter) for t in range(per)], axis=1
        )
        ready.append((x_from, g_from, act, dpre))

    for c in range(chunks):
        cols = pl.ds(c * step_w, step_w)
        grad_in, grad_out = 0.0, 0.0
        for x_from, g_from, act, dpre in ready:
            x_cols = x_from[:, :, cols].reshape(micro * rows, step_w)
            g_cols = g_from[:, :, cols].reshape(micro * rows, step_w)
            grad_in = grad_in + dot(x_cols, dpre, FIRST)
            grad_out = grad_out + dot(act, g_cols, FIRST)
        pin_ref[cols, :] = grad_in.astype(jnp.bfloat16)
        pout_ref[:, cols] = grad_out.astype(jnp.bfloat16)

    for copy in pre_copies + act_copies:
        copy.wait_send()
    if pair:
        for copy in [wi_copy, wo_copy, x_copy, actx_copy] + gx_copies + dx_copies:
            copy.wait_send()
    for m in range(micro):
        for copy in hid_copies[m] + dp_copies[m]:
            copy.wait_send()

        @pl.when(section > 0)
        def _():
            for copy in g_copies[m]:
                copy.wait_send()


def shards(acts, w_in, w_out, top_grad):
    pipes = lax.axis_size("pipe")
    parts = lax.axis_size("tensor")
    pair = lax.axis_size("dp") == 2 and parts % 2 == 0
    saved = acts[0]
    micro, rows, width = saved.shape
    if pair:
        w_in_now, w_out_now = w_in[0], w_out[0]
    else:
        w_in_now = lax.all_gather(w_in[0], "dp", axis=1, tiled=True)
        w_out_now = lax.all_gather(w_out[0], "dp", axis=0, tiled=True)
    own = w_in_now.shape[1]
    per = parts // 2 if pair else parts
    quarter = own // per
    chunks = 4
    others = parts - 1
    bf, f32 = jnp.bfloat16, jnp.float32
    dma = pltpu.SemaphoreType.DMA
    vmem = pl.BlockSpec(memory_space=pltpu.VMEM)
    across = []
    if pair:
        across = [
            pltpu.VMEM((width, own), bf),
            pltpu.VMEM((own, width), bf),
            pltpu.VMEM((micro, rows, width), bf),
            pltpu.VMEM((micro, rows, width), bf),
            pltpu.VMEM((micro, per, rows, quarter), bf),
            pltpu.VMEM((per, micro * rows, quarter), bf),
            dma((4,)), dma((4,)),
            dma((micro,)), dma((micro,)), dma((micro,)), dma((micro,)),
        ]
    back, grad_in, grad_out = pl.pallas_call(
        functools.partial(chain, pipes, parts, pair, chunks),
        out_shape=(
            jax.ShapeDtypeStruct((micro, rows, width), bf),
            jax.ShapeDtypeStruct((width, own), bf),
            jax.ShapeDtypeStruct((own, width), bf),
        ),
        in_specs=[vmem] * 4,
        out_specs=(vmem,) * 3,
        scratch_shapes=[
            pltpu.VMEM((micro, rows, width), bf),
            pltpu.VMEM((parts, micro * rows, quarter), f32),
            pltpu.VMEM((others, micro * rows, quarter), f32),
            pltpu.VMEM((parts, micro * rows, quarter), bf),
            pltpu.VMEM((micro, parts, rows, quarter), f32),
            pltpu.VMEM((micro, others, rows, quarter), f32),
            pltpu.VMEM((micro, parts, rows, quarter), bf),
            pltpu.VMEM((micro * rows, quarter), f32),
            dma((others,)), dma((others,)), dma((others,)), dma((others,)),
            dma((micro, others)), dma((micro, others)),
            dma((micro, others)), dma((micro, others)),
            dma((micro, chunks)), dma((micro, chunks)),
            *across,
        ],
        compiler_params=pltpu.CompilerParams(
            collective_id=0, has_side_effects=True, vmem_limit_bytes=48 * 1024 * 1024
        ),
    )(saved, w_in_now, w_out_now, top_grad)
    if not pair:
        grad_in = lax.psum_scatter(grad_in, "dp", scatter_dimension=1, tiled=True)
        grad_out = lax.psum_scatter(grad_out, "dp", scatter_dimension=0, tiled=True)
    return back[None], grad_in[None], grad_out[None]


def solution(mesh):
    placed = (
        P("pipe", None, "dp", "tensor"),
        P("pipe", "tensor", "dp"),
        P("pipe", "dp", "tensor"),
        P(None, "dp", "tensor"),
    )
    return jax.shard_map(
        shards,
        mesh=mesh,
        in_specs=placed,
        out_specs=(
            P("pipe", None, "dp", "tensor"),
            P("pipe", "tensor", "dp"),
            P("pipe", "dp", "tensor"),
        ),
        check_vma=False,
    )
```

time: 245 us -> 143 us (0.58)
  waiting for transfers between devices: 136 us -> 0 us
  Pallas kernels: 93.3 us -> 137 us
  between operations: 13.8 us -> 0.65 us
  local copies, waits for them, and re-layouts: 0.98 us -> 5.35 us
    all_gather x2 -> x0, waiting for transfers between devices: 71.3 us -> none  [the longest x1 36.7 us: shards(): w_in_full = lax.all_gather(w_in[0], 'dp', axis=1, tiled=True)]
    reduce_scatter x2 -> x0, waiting for transfers between devices: 62.9 us -> none  [the longest x1 34.6 us: shards(): grad_out = lax.psum_scatter(part_out, 'dp', scatter_dimension=0, tiled=True)]
    pallas_call x1, Pallas kernels: 93.3 us -> 137 us  [shards(): pl.pallas_call(functools.partial(chain, pipes, parts, pair, chunks), out_...]
    unnamed x5 -> x7, local copies, waits for them, and re-layouts: 0.98 us -> 5.35 us
  transfers between devices with their start and end apart: 4 -> 0, of which waited for: 4 -> 0; matrix products, arithmetic and copies ran while one was open for 0% -> 0% of each run, Pallas kernels for 0% -> 0%
where the time goes in v2:
time: 143 us
  Pallas kernels  137 us (96%)
  local copies, waits for them, and re-layouts  5.35 us (4%)
    pallas_call x1, Pallas kernels, shards(): pl.pallas_call(functools.partial(chain, pipes, parts, pair, chunks), out_...  137 us
    unnamed x7, local copies, waits for them, and re-layouts  5.35 us

profile of v2, /device:TPU:0, one launch (start us, length us, event | category | flops | bytes accessed | tf_op | source)
XLA Modules:
  0.0 142.7 jit_solution(16712845084092248828)
XLA Ops:
  0.6 0.0 copy-start
  0.6 1.2 copy-done
  1.9 0.0 copy-start.1
  1.9 1.2 copy-done.1
  3.1 136.7 %shard_map.67 = (bf16[4,64,2048]{2,1,0:T(8,128)(2,1)S(1)}, bf16[2048,256]{1,0:T(8,128)(2,1)S(1)}, bf16[256,2048]{1,0:T(8,128)(2,1)S(1)}) custom-call(bf16[4,64,2048]{2,1,0:T(8,128)(2,1)S(1)} %bitcast.9, bf16[2048,256]{1,0:T(8,128)(2,1)S(1)} %bitcast.10, bf16[256,2048]{1,0:T(8,128)(2,1)} %bitcast.11, bf16[4,64,2048]{2,1,0:T(8,128)(2,1)} %top_ref.1), custom_call_target="tpu_custom_call" | custom-call | tf_op jit(solution)/shard_map/pallas_call | solution.py:283
  139.8 1.0 copy.10
  140.8 1.0 copy.11
  141.7 1.0 copy.12
Async XLA Ops:
  0.6 1.2 copy-start
  1.9 1.2 copy-start.1

commit v3 on v2

--- a/solution.py
+++ b/solution.py
@@ -46,8 +46,10 @@
     for peer in peers:
         pl.semaphore_signal(barrier, inc=1, device_id={"tensor": peer}, device_id_type=MESH)
     if pair:
-        partner = {"dp": 1 - lax.axis_index("dp")}
-        pl.semaphore_signal(barrier, inc=1, device_id=partner, device_id_type=MESH)
+        other_dp = 1 - lax.axis_index("dp")
+        partner = {"dp": other_dp}
+        for t in range(parts):
+            pl.semaphore_signal(barrier, inc=1, device_id={"dp": other_dp, "tensor": t}, device_id_type=MESH)
 
     @pl.when(section > 0)
     def _():
@@ -58,7 +60,7 @@
         pl.semaphore_signal(barrier, inc=1, device_id={"pipe": above}, device_id_type=MESH)
 
     beside = jnp.minimum(section, 1) + jnp.minimum(pipes - 1 - section, 1)
-    pl.semaphore_wait(barrier, parts - 1 + halves - 1 + beside)
+    pl.semaphore_wait(barrier, parts - 1 + (halves - 1) * parts + beside)
 
     def remote(src, dst, send, recv, where):
         return pltpu.make_async_remote_copy(
@@ -68,7 +70,7 @@
 
     wi_halves, wo_halves = [wi_ref], [wo_ref]
     if pair:
-        wi_other, wo_other, x_other, g_other, dpre_other, act_other, one_ss, one_rs, gx_ss, gx_rs, dx_ss, dx_rs = across
+        wi_other, wo_other, x_other, g_other, dpre_other, act_other, one_ss, one_rs, gx_ss, gx_rs, dx_ss, dx_rs, top_recv, top_ss, top_rs = across
         wi_halves.append(wi_other)
         wo_halves.append(wo_other)
         wi_copy = remote(wi_ref, wi_other, one_ss.at[0], one_rs.at[0], partner)
@@ -123,37 +125,112 @@
     for h in range(halves):
         if h == 1:
             wi_copy.wait_recv()
-            wo_copy.start()
+
+            @pl.when(first)
+            def _():
+                gx_copies[0].start()
+
+            @pl.when(section < pipes - 1)
+            def _():
+                wo_copy.start()
+
         pre = jnp.dot(flat_x, wi_halves[h][...], preferred_element_type=jnp.float32)
         for t in range(per):
             pre_send[h * per + t] = pre[:, t * quarter : (t + 1) * quarter]
     for copy in pre_copies:
         copy.start()
 
-    def hidden_now(which):
-        count = len(which)
-        g_now = g_buf[which[0] : which[-1] + 1].reshape(count * rows, width)
+    def top_copy(m, q):
+        where = {"tensor": q} if q < per else {"dp": other_dp, "tensor": q}
+        return remote(hid_send.at[m, q], top_recv.at[m, me], top_ss.at[m, q], top_rs.at[m, me], where)
+
+    def top_wait(m, t):
+        return remote(hid_send.at[m, t], top_recv.at[m, t], top_ss.at[m, t], top_rs.at[m, t], {"tensor": peers[0]})
+
+    def hidden_top(m):
+        gx_copies[m].wait_recv()
+        if m + 1 < micro:
+            gx_copies[m + 1].start()
+        else:
+            x_copy.start()
+        part = dot(jnp.concatenate([g_buf[m], g_other[m]], axis=0), wo_ref[...], LAST)
+        for q in range(parts):
+            at = (q % per) * quarter
+            low = 0 if q < per else rows
+            hid_send[m, q] = part[low : low + rows, at : at + quarter]
+            if q < per:
+                @pl.when(me == q)
+                def _():
+                    top_recv[m, q] = part[low : low + rows, at : at + quarter]
+
+                @pl.when(me != q)
+                def _():
+                    top_copy(m, q).start()
+            else:
+                top_copy(m, q).start()
+
+    def hidden_chain(m):
         for h in range(halves):
-            part = dot(g_now, wo_halves[h][...], LAST)
+            part = dot(g_buf[m], wo_halves[h][...], LAST)
             for t in range(per):
-                for i, m in enumerate(which):
-                    hid_send[m, h * per + t] = part[i * rows : (i + 1) * rows, t * quarter : (t + 1) * quarter]
-        for m in which:
-            for copy in hid_copies[m]:
-                copy.start()
+                hid_send[m, h * per + t] = part[:, t * quarter : (t + 1) * quarter]
+        for copy in hid_copies[m]:
+            copy.start()
         if pair:
-            for m in which:
-                gx_copies[m].start()
-
-    def dpre_now(m):
+            gx_copies[m].start()
+
+    def hidden_now(m):
+        @pl.when(first)
+        def _():
+            if pair:
+                hidden_top(m)
+            else:
+                hidden_chain(m)
+
+        @pl.when(section < pipes - 1)
+        def _():
+            for copy in g_copies[m]:
+                copy.wait_recv()
+            hidden_chain(m)
+
+    def dpre_finish(m, hidden):
+        dpre_buf[m, me] = (hidden * slope_buf[m * rows : (m + 1) * rows, :]).astype(jnp.bfloat16)
+        for copy in dp_copies[m]:
+            copy.start()
+
+    def dpre_chain(m):
         for copy in hid_copies[m]:
             copy.wait_recv()
         hidden = hid_send[m, me]
         for d in range(parts - 1):
             hidden = hidden + hid_recv[m, d]
-        dpre_buf[m, me] = (hidden * slope_buf[m * rows : (m + 1) * rows, :]).astype(jnp.bfloat16)
-        for copy in dp_copies[m]:
-            copy.start()
+        dpre_finish(m, hidden)
+
+    def dpre_top(m):
+        for t in range(parts):
+            if t < per:
+                @pl.when(me != t)
+                def _():
+                    top_wait(m, t).wait_recv()
+            else:
+                top_wait(m, t).wait_recv()
+        hidden = top_recv[m, 0]
+        for t in range(1, parts):
+            hidden = hidden + top_recv[m, t]
+        dpre_finish(m, hidden)
+
+    def dpre_now(m):
+        if not pair:
+            dpre_chain(m)
+            return
+
+        @pl.when(first)
+        def _():
+            dpre_top(m)
+
+        @pl.when(section < pipes - 1)
+        def _():
+            dpre_chain(m)
 
     for copy in pre_copies:
         copy.wait_recv()
@@ -166,23 +243,16 @@
         copy.start()
 
     if pair:
-        wo_copy.wait_recv()
-        x_copy.start()
-
-    @pl.when(first)
-    def _():
-        hidden_now(list(range(micro)))
-        for m in range(micro):
-            dpre_now(m)
-
+        @pl.when(section < pipes - 1)
+        def _():
+            wo_copy.wait_recv()
+            x_copy.start()
+
+    hidden_now(0)
     for m in range(micro):
-        @pl.when(section < pipes - 1)
-        def _():
-            for copy in g_copies[m]:
-                copy.wait_recv()
-            hidden_now([m])
-            dpre_now(m)
-
+        dpre_now(m)
+        if m + 1 < micro:
+            hidden_now(m + 1)
         for copy in dp_copies[m]:
             copy.wait_recv()
         dpre_halves = [
@@ -212,7 +282,10 @@
         x_copy.wait_recv()
         actx_copy.wait_recv()
         for m in range(micro):
-            gx_copies[m].wait_recv()
+            @pl.when(section < pipes - 1)
+            def _():
+                gx_copies[m].wait_recv()
+
             dx_copies[m].wait_recv()
         sources.append((x_other, g_other, act_other, dpre_other))
     ready = []
@@ -237,10 +310,32 @@
     for copy in pre_copies + act_copies:
         copy.wait_send()
     if pair:
-        for copy in [wi_copy, wo_copy, x_copy, actx_copy] + gx_copies + dx_copies:
+        for copy in [wi_copy, x_copy, actx_copy] + gx_copies + dx_copies:
             copy.wait_send()
+
+        @pl.when(first)
+        def _():
+            for m in range(micro):
+                for q in range(parts):
+                    if q < per:
+                        @pl.when(me != q)
+                        def _():
+                            top_copy(m, q).wait_send()
+                    else:
+                        top_copy(m, q).wait_send()
+
+        @pl.when(section < pipes - 1)
+        def _():
+            wo_copy.wait_send()
+            for m in range(micro):
+                for copy in hid_copies[m]:
+                    copy.wait_send()
+    else:
+        for m in range(micro):
+            for copy in hid_copies[m]:
+                copy.wait_send()
     for m in range(micro):
-        for copy in hid_copies[m] + dp_copies[m]:
+        for copy in dp_copies[m]:
             copy.wait_send()
 
         @pl.when(section > 0)
@@ -279,6 +374,8 @@
             pltpu.VMEM((per, micro * rows, quarter), bf),
             dma((4,)), dma((4,)),
             dma((micro,)), dma((micro,)), dma((micro,)), dma((micro,)),
+            pltpu.VMEM((micro, parts, rows, quarter), f32),
+            dma((micro, parts)), dma((micro, parts)),
         ]
     back, grad_in, grad_out = pl.pallas_call(
         functools.partial(chain, pipes, parts, pair, chunks),

time: 143 us -> 153 us (1.070)
  Pallas kernels: 137 us -> 147 us
    pallas_call x1, Pallas kernels: 137 us -> 147 us  [shards(): pl.pallas_call(functools.partial(chain, pipes, parts, pair, chunks), out_...]
where the time goes in v3:
time: 153 us
  Pallas kernels  147 us (96%)
  local copies, waits for them, and re-layouts  5.35 us (3%)
    pallas_call x1, Pallas kernels, shards(): pl.pallas_call(functools.partial(chain, pipes, parts, pair, chunks), out_...  147 us
    unnamed x7, local copies, waits for them, and re-layouts  5.35 us

profile of v3, /device:TPU:0, one launch (start us, length us, event | category | flops | bytes accessed | tf_op | source)
XLA Modules:
  0.0 152.6 jit_solution(17340839260426767536)
XLA Ops:
  0.6 0.0 copy-start
  0.6 1.2 copy-done
  1.9 0.0 copy-start.1
  1.9 1.2 copy-done.1
  3.1 146.6 %shard_map.67 = (bf16[4,64,2048]{2,1,0:T(8,128)(2,1)S(1)}, bf16[2048,256]{1,0:T(8,128)(2,1)S(1)}, bf16[256,2048]{1,0:T(8,128)(2,1)S(1)}) custom-call(bf16[4,64,2048]{2,1,0:T(8,128)(2,1)S(1)} %bitcast.9, bf16[2048,256]{1,0:T(8,128)(2,1)S(1)} %bitcast.10, bf16[256,2048]{1,0:T(8,128)(2,1)} %bitcast.11, bf16[4,64,2048]{2,1,0:T(8,128)(2,1)} %top_ref.1), custom_call_target="tpu_custom_call" | custom-call | tf_op jit(solution)/shard_map/pallas_call | solution.py:380
  149.7 1.0 copy.10
  150.7 1.0 copy.11
  151.6 1.0 copy.12
Async XLA Ops:
  0.6 1.2 copy-start
  1.9 1.2 copy-start.1

commit v4 on v3

--- a/solution.py
+++ b/solution.py
@@ -248,11 +248,9 @@
             wo_copy.wait_recv()
             x_copy.start()
 
-    hidden_now(0)
     for m in range(micro):
+        hidden_now(m)
         dpre_now(m)
-        if m + 1 < micro:
-            hidden_now(m + 1)
         for copy in dp_copies[m]:
             copy.wait_recv()
         dpre_halves = [

time: 153 us -> 168 us (1.098)
  Pallas kernels: 147 us -> 162 us
    pallas_call x1, Pallas kernels: 147 us -> 162 us  [shards(): pl.pallas_call(functools.partial(chain, pipes, parts, pair, chunks), out_...]
where the time goes in v4:
time: 168 us
  Pallas kernels  162 us (96%)
  local copies, waits for them, and re-layouts  5.35 us (3%)
    pallas_call x1, Pallas kernels, shards(): pl.pallas_call(functools.partial(chain, pipes, parts, pair, chunks), out_...  162 us
    unnamed x7, local copies, waits for them, and re-layouts  5.35 us

profile of v4, /device:TPU:0, one launch (start us, length us, event | category | flops | bytes accessed | tf_op | source)
XLA Modules:
  0.0 167.8 jit_solution(15855150540543716807)
XLA Ops:
  0.6 0.0 copy-start
  0.6 1.2 copy-done
  1.9 0.0 copy-start.1
  1.9 1.2 copy-done.1
  3.1 161.8 %shard_map.67 = (bf16[4,64,2048]{2,1,0:T(8,128)(2,1)S(1)}, bf16[2048,256]{1,0:T(8,128)(2,1)S(1)}, bf16[256,2048]{1,0:T(8,128)(2,1)S(1)}) custom-call(bf16[4,64,2048]{2,1,0:T(8,128)(2,1)S(1)} %bitcast.9, bf16[2048,256]{1,0:T(8,128)(2,1)S(1)} %bitcast.10, bf16[256,2048]{1,0:T(8,128)(2,1)} %bitcast.11, bf16[4,64,2048]{2,1,0:T(8,128)(2,1)} %top_ref.1), custom_call_target="tpu_custom_call" | custom-call | tf_op jit(solution)/shard_map/pallas_call | solution.py:378
  164.9 1.0 copy.10
  165.8 1.0 copy.11
  166.8 1.0 copy.12
Async XLA Ops:
  0.6 1.2 copy-start
  1.9 1.2 copy-start.1
